TPU v7x, 32 devices: a whole 2x2x4 slice. The times are simulated.
32 devices in a mesh: pat: 4 (over z), vox: 8 (over y, x, core).
Axes of the slice: x: 2, y: 2, z: 4, core: 2. Of those that a mesh axis runs over, the one named last changes fastest.
Arguments:
- conductivity: float32 [16, 128, 128], P('vox'), may hold values from 0.3 to 1.5
- warm_forward: float32 [16, 32, 128, 128], P('vox', 'pat'), may hold values from -3 to 3
- warm_adjoint: float32 [16, 32, 128, 128], P('vox', 'pat'), may hold values from -3 to 3
- electrodes: int32 [128], replicated, may hold values from 0 to 262143
- patterns: int32 [32, 4], P('pat'), may hold values from 0 to 127, all different within a row
- observed: float32 [32], P('pat'), may hold values from -16 to 16
Outputs:
- gradient: float32 [16, 128, 128], P('vox')
- predicted: float32 [32], P('pat')
All inputs are finite; a program needn't handle non-finite values.
Results may differ from a plain program's by a relative error of at most 0.0003.
Values sent between devices are 32-bit elements; how exact they have to be, the bound alone decides.
No kernel may reach another device: no remote copies, remote signals or barrier semaphores. Data moves between devices by JAX's collectives and lax.ppermute only.
A program may use at most 64 MiB of HBM per device.

v0:
```python
import math
import jax
import jax.numpy as jnp
from jax import lax
from jax.sharding import PartitionSpec as P

ITERS = 2
leakage = 0.05


def extended(block, sides, width):
    for axis, dim in sides:
        count = lax.axis_size(axis)
        forward = [(i, i + 1) for i in range(count - 1)]
        backward = [(target, source) for source, target in forward]
        low = lax.ppermute(
            lax.slice_in_dim(block, block.shape[dim] - width, None, axis=dim), axis, forward
        )
        high = lax.ppermute(lax.slice_in_dim(block, 0, width, axis=dim), axis, backward)
        block = jnp.concatenate([low, block, high], axis=dim)
    return block


def both_sides(values, along_axis):
    lower_pad = [(0, 0)] * values.ndim
    upper_pad = [(0, 0)] * values.ndim
    lower_pad[along_axis] = (1, 0)
    upper_pad[along_axis] = (0, 1)
    return jnp.pad(values, lower_pad) + jnp.pad(values, upper_pad)


def spread(values, along_axis):
    lower_pad = [(0, 0)] * values.ndim
    upper_pad = [(0, 0)] * values.ndim
    lower_pad[along_axis] = (1, 0)
    upper_pad[along_axis] = (0, 1)
    return jnp.pad(values, lower_pad) - jnp.pad(values, upper_pad)


def operate(values, coeffs):
    depth_faces, row_faces, column_faces = coeffs
    padded = extended(values, (("vox", 0),), 1)
    flux_depth = depth_faces[:, None] * (padded[1:] - padded[:-1])
    result = leakage * values + (flux_depth[:-1] - flux_depth[1:])
    result = result + spread(row_faces[:, None] * (values[:, :, 1:] - values[:, :, :-1]), 2)
    result = result + spread(
        column_faces[:, None] * (values[:, :, :, 1:] - values[:, :, :, :-1]), 3
    )
    return result


def inner(left_factor, right_factor):
    return jnp.sum(left_factor * right_factor, axis=(0, 2, 3))


def widen(vector):
    return vector[None, :, None, None]


def pattern_sum(local_terms):
    return lax.psum(local_terms, "vox")


def solve_pattern(right_side, initial, coeffs, diagonal):
    solution = initial
    residue = right_side - operate(solution, coeffs)
    precond = residue / diagonal
    direction = precond
    current = pattern_sum(inner(residue, precond))
    for iteration in range(ITERS):
        applied = operate(direction, coeffs)
        step_size = current / pattern_sum(inner(direction, applied))
        solution = solution + widen(step_size) * direction
        residue = residue - widen(step_size) * applied
        if iteration + 1 < ITERS:
            precond = residue / diagonal
            following = pattern_sum(inner(residue, precond))
            direction = precond + widen(following / current) * direction
            current = following
    return solution


def per_device(conductivity, warm_forward, warm_adjoint, electrodes, patterns, observed):
    plane_count, pattern_count, row_count, column_count = warm_forward.shape
    position = lax.axis_index("vox")
    layers = lax.axis_size("vox")
    strength = 2.0 * math.sqrt(layers * plane_count * row_count * column_count)
    data_weight = 0.1 * strength
    lower_open = (position > 0).astype(jnp.float32)
    upper_open = (position < layers - 1).astype(jnp.float32)
    padded_sigma = extended(conductivity, (("vox", 0),), 1)
    face_mask = jnp.concatenate(
        [lower_open[None], jnp.ones((plane_count - 1,), jnp.float32), upper_open[None]]
    )
    depth_faces = 0.5 * (padded_sigma[1:] + padded_sigma[:-1]) * face_mask[:, None, None]
    row_faces = 0.5 * (conductivity[:, 1:] + conductivity[:, :-1])
    column_faces = 0.5 * (conductivity[:, :, 1:] + conductivity[:, :, :-1])
    coeffs = (depth_faces, row_faces, column_faces)
    diagonal = (
        leakage
        + (depth_faces[:-1] + depth_faces[1:])
        + both_sides(row_faces, 1)
        + both_sides(column_faces, 2)
    )
    diagonal = diagonal[:, None]
    electrode_ids = jnp.arange(electrodes.shape[0], dtype=jnp.int32)
    picked = jnp.sum(
        jnp.where(
            patterns[:, :, None] == electrode_ids[None, None, :], electrodes[None, None, :], 0
        ),
        axis=2,
    )
    offset = position * (plane_count * row_count * column_count)
    local_cell = picked - offset
    grid_shape = (plane_count, 1, row_count, column_count)
    cell_index = (
        lax.broadcasted_iota(jnp.int32, grid_shape, 0) * row_count
        + lax.broadcasted_iota(jnp.int32, grid_shape, 2)
    ) * column_count + lax.broadcasted_iota(jnp.int32, grid_shape, 3)

    def marker(which_one):
        return (cell_index == local_cell[:, which_one][None, :, None, None]).astype(jnp.float32)

    forward = solve_pattern(strength * (marker(0) - marker(1)), warm_forward, coeffs, diagonal)
    probe_weights = marker(2) - marker(3)
    predicted = lax.psum(inner(probe_weights, forward), "vox")
    misfit = predicted - observed
    adjoint = solve_pattern(
        widen(data_weight * misfit) * probe_weights, warm_adjoint, coeffs, diagonal
    )
    stacked = jnp.concatenate([forward, adjoint], axis=1)
    padded_pair = extended(stacked, (("vox", 0),), 1)
    padded_forward = padded_pair[:, :pattern_count]
    padded_adjoint = padded_pair[:, pattern_count:]
    depth_products = jnp.sum(
        (padded_forward[1:] - padded_forward[:-1]) * (padded_adjoint[1:] - padded_adjoint[:-1]),
        axis=1,
    )
    depth_products = depth_products * face_mask[:, None, None]
    grad_depth = depth_products[:-1] + depth_products[1:]
    row_products = jnp.sum(
        (forward[:, :, 1:] - forward[:, :, :-1]) * (adjoint[:, :, 1:] - adjoint[:, :, :-1]), axis=1
    )
    column_products = jnp.sum(
        (forward[:, :, :, 1:] - forward[:, :, :, :-1])
        * (adjoint[:, :, :, 1:] - adjoint[:, :, :, :-1]),
        axis=1,
    )
    local_gradient = -0.5 * (
        grad_depth + both_sides(row_products, 1) + both_sides(column_products, 2)
    )
    gradient = lax.psum(local_gradient, "pat")
    return (gradient, predicted)


def solution(mesh):
    in_specs = (
        P("vox", None, None),
        P("vox", "pat", None, None),
        P("vox", "pat", None, None),
        P(),
        P("pat", None),
        P("pat"),
    )
    out_specs = (P("vox", None, None), P("pat"))
    return jax.shard_map(
        per_device, mesh=mesh, in_specs=in_specs, out_specs=out_specs, check_vma=False
    )
```

profile of v0, /device:TPU:0, one launch (start us, length us, event | category | flops | bytes accessed | tf_op | source)
XLA Modules:
  0.0 282.5 jit_solution(13601715273596078150)
XLA Ops:
  7.2 1.0 fusion.63
  8.2 1.3 collective-permute-start
  9.5 3.0 %collective-permute-start.1 = (f32[1,128,128]{2,1,0:T(8,128)S(1)}, f32[1,128,128]{2,1,0:T(8,128)S(1)}, u32[]{:S(2)}, u32[]{:S(2)}) collective-permute-start(f32[1,128,128]{2,1,0:T(8,128)S(1)} %get-tuple-element.42), channel_id=1, source_target_pairs={{0,1},{1,2},{2,3},{3,4},{4,5},{5,6},{6,7},{8,9},{9,10},{10,11},{11... | collective-permute-start | bytes 196616 | tf_op jit(solution)/shard_map/ppermute | solution.py:16
  12.5 2.1 fusion.61
  14.6 1.4 collective-permute-start.2
  16.1 5.9 %collective-permute-start.3 = (f32[1,8,128,128]{3,2,1,0:T(8,128)S(1)}, f32[1,8,128,128]{3,2,1,0:T(8,128)}, u32[]{:S(2)}, u32[]{:S(2)}) collective-permute-start(f32[1,8,128,128]{3,2,1,0:T(8,128)S(1)} %get-tuple-element.32), channel_id=1, source_target_pairs={{0,1},{1,2},{2,3},{3,4},{4,5},{5,6},{6,7},{8,9},{9,10},{10,11},{11... | collective-permute-start | bytes 1572872 | tf_op jit(solution)/shard_map/ppermute | solution.py:16
  22.0 1.1 fusion.62
  23.1 3.7 %collective-permute-start.9 = (f32[1,8,128,128]{3,2,1,0:T(8,128)}, f32[1,8,128,128]{3,2,1,0:T(8,128)}, u32[]{:S(2)}, u32[]{:S(2)}) collective-permute-start(f32[1,8,128,128]{3,2,1,0:T(8,128)} %get-tuple-element.34), channel_id=1, source_target_pairs={{0,1},{1,2},{2,3},{3,4},{4,5},{5,6},{6,7},{8,9},{9,10},{10,11},{11... | collective-permute-start | bytes 1572872 | tf_op jit(solution)/shard_map/ppermute | solution.py:16
  26.9 0.7 iota_add_fusion
  27.6 0.2 select_reduce_fusion
  27.9 0.3 subtract_multiply_fusion.2
  28.7 1.4 fusion.2
  30.1 0.8 broadcast_divide_fusion.1
  31.0 1.4 collective-permute-start.4
  32.5 3.3 %collective-permute-start.5 = (f32[1,8,128,128]{3,2,1,0:T(8,128)S(1)}, f32[1,8,128,128]{3,2,1,0:T(8,128)S(1)}, u32[]{:S(2)}, u32[]{:S(2)}) collective-permute-start(f32[1,8,128,128]{3,2,1,0:T(8,128)S(1)} %get-tuple-element.30), channel_id=1, source_target_pairs={{0,1},{1,2},{2,3},{3,4},{4,5},{5,6},{6,7},{8,9},{9,10},{10,11},{11... | collective-permute-start | bytes 1572872 | tf_op jit(solution)/shard_map/ppermute | solution.py:16
  35.8 0.3 fusion.36
  36.4 1.0 collective-permute-done.5
  37.3 0.2 fusion.3
  37.5 1.7 multiply_reduce_fusion.5
  39.2 27.2 %all-reduce.33 = (f32[8]{0:T(128)S(1)}, f32[8]{0:T(128)S(1)}) all-reduce(f32[8]{0:T(128)S(1)} %get-tuple-element.5, f32[8]{0:T(128)S(1)} %get-tuple-element.4), channel_id=1, replica_groups=mesh['pat'=4,'vox'=8] {'vox'}, use_global_device_ids=true, to_apply=%region_2.3 | all-reduce | flops 16 | bytes 128 | tf_op jit(solution)/shard_map/psum | solution.py:61
  66.5 1.6 multiply_reduce_fusion.4
  68.0 1.3 collective-permute-start.8
  69.3 15.8 %psum.72 = f32[8]{0:T(128)S(1)} all-reduce(f32[8]{0:T(128)S(1)} %multiply_reduce_fusion.4), channel_id=1, replica_groups=mesh['pat'=4,'vox'=8] {'vox'}, use_global_device_ids=true, to_apply=%region_6.7 | all-reduce | flops 8 | bytes 64 | tf_op jit(solution)/shard_map/psum | solution.py:61
  85.2 1.8 multiply_add_fusion.3
  87.1 1.3 collective-permute-start.6
  88.4 3.2 %collective-permute-start.7 = (f32[1,8,128,128]{3,2,1,0:T(8,128)S(1)}, f32[1,8,128,128]{3,2,1,0:T(8,128)S(1)}, u32[]{:S(2)}, u32[]{:S(2)}) collective-permute-start(f32[1,8,128,128]{3,2,1,0:T(8,128)S(1)} %get-tuple-element.28), channel_id=1, source_target_pairs={{0,1},{1,2},{2,3},{3,4},{4,5},{5,6},{6,7},{8,9},{9,10},{10,11},{11... | collective-permute-start | bytes 1572872 | tf_op jit(solution)/shard_map/ppermute | solution.py:16
  91.6 1.6 fusion.29
  93.2 1.3 fusion.30
  94.5 2.8 fusion.4
  97.3 0.7 fusion.35
  98.0 20.6 %psum.73 = f32[8]{0:T(128)S(1)} all-reduce(f32[8]{0:T(128)S(1)} %fusion.35), channel_id=1, replica_groups=mesh['pat'=4,'vox'=8] {'vox'}, use_global_device_ids=true, to_apply=%region_8.9 | all-reduce | flops 8 | bytes 64 | tf_op jit(solution)/shard_map/psum | solution.py:61
  118.6 2.8 multiply_reduce_fusion.3
  121.4 12.4 %psum.74 = f32[8]{0:T(128)S(1)} all-reduce(f32[8]{0:T(128)S(1)} %get-tuple-element.15), channel_id=1, replica_groups=mesh['pat'=4,'vox'=8] {'vox'}, use_global_device_ids=true, to_apply=%region_10.11 | all-reduce | flops 8 | bytes 64 | tf_op jit(solution)/shard_map/psum | solution.py:126
  133.9 3.7 %broadcast_divide_fusion = (f32[2,8,128,128]{3,2,1,0:T(8,128)S(1)}, f32[2,8,128,128]{3,2,1,0:T(8,128)S(1)}) fusion(f32[2,128,128]{2,1,0:T(8,128)S(1)} %fusion.51, f32[2,8,128,127]{3,2,1,0:T(8,128)} %get-tuple-element.41, f32[2,8,127,128]{3,2,1,0:T(8,128)} %get-tuple-element.39, f32[3,8,128,128]{3,2,1,0:T(8,128)} %get-tuple-element.37, ...), kind=kLoop, calls=%fused_computation.94 | loop fusion | flops 3932160 | bytes 7585888 | tf_op jit(solution)/shard_map/div | solution.py:67
  137.7 1.3 collective-permute-start.10
  139.0 3.2 %collective-permute-start.11 = (f32[1,8,128,128]{3,2,1,0:T(8,128)S(1)}, f32[1,8,128,128]{3,2,1,0:T(8,128)S(1)}, u32[]{:S(2)}, u32[]{:S(2)}) collective-permute-start(f32[1,8,128,128]{3,2,1,0:T(8,128)S(1)} %get-tuple-element.26), channel_id=1, source_target_pairs={{0,1},{1,2},{2,3},{3,4},{4,5},{5,6},{6,7},{8,9},{9,10},{10,11},{11... | collective-permute-start | bytes 1572872 | tf_op jit(solution)/shard_map/ppermute | solution.py:16
  142.2 0.3 fusion.20
  142.8 1.0 collective-permute-done.11
  143.7 0.2 fusion.6
  143.9 0.8 multiply_reduce_fusion.1
  144.7 20.3 %all-reduce.32 = (f32[8]{0:T(128)S(1)}, f32[8]{0:T(128)S(1)}) all-reduce(f32[8]{0:T(128)S(1)} %get-tuple-element.3, f32[8]{0:T(128)S(1)} %get-tuple-element.2), channel_id=1, replica_groups=mesh['pat'=4,'vox'=8] {'vox'}, use_global_device_ids=true, to_apply=%region_12.13 | all-reduce | flops 16 | bytes 128 | tf_op jit(solution)/shard_map/psum | solution.py:61
  165.0 0.3 multiply_reduce_fusion
  165.4 12.6 %psum.77 = f32[8]{0:T(128)S(1)} all-reduce(f32[8]{0:T(128)S(1)} %multiply_reduce_fusion), channel_id=1, replica_groups=mesh['pat'=4,'vox'=8] {'vox'}, use_global_device_ids=true, to_apply=%region_16.17 | all-reduce | flops 8 | bytes 64 | tf_op jit(solution)/shard_map/psum | solution.py:61
  178.0 1.5 multiply_add_fusion.1
  179.6 1.3 collective-permute-start.12
  180.9 3.2 %collective-permute-start.13 = (f32[1,8,128,128]{3,2,1,0:T(8,128)S(1)}, f32[1,8,128,128]{3,2,1,0:T(8,128)S(1)}, u32[]{:S(2)}, u32[]{:S(2)}) collective-permute-start(f32[1,8,128,128]{3,2,1,0:T(8,128)S(1)} %get-tuple-element.24), channel_id=1, source_target_pairs={{0,1},{1,2},{2,3},{3,4},{4,5},{5,6},{6,7},{8,9},{9,10},{10,11},{11... | collective-permute-start | bytes 1572872 | tf_op jit(solution)/shard_map/ppermute | solution.py:16
  184.1 0.3 fusion.13
  184.7 1.0 collective-permute-done.13
  185.6 0.2 fusion.7
  185.8 0.7 fusion.19
  186.5 20.7 %psum.78 = f32[8]{0:T(128)S(1)} all-reduce(f32[8]{0:T(128)S(1)} %fusion.19), channel_id=1, replica_groups=mesh['pat'=4,'vox'=8] {'vox'}, use_global_device_ids=true, to_apply=%region_18.19 | all-reduce | flops 8 | bytes 64 | tf_op jit(solution)/shard_map/psum | solution.py:61
  207.2 0.3 multiply_add_fusion
  207.5 0.9 copy-done.2
  208.5 0.2 fusion.8
  208.7 1.3 collective-permute-start.14
  210.0 3.1 %collective-permute-start.15 = (f32[1,16,128,128]{3,2,1,0:T(8,128)S(1)}, f32[1,16,128,128]{3,2,1,0:T(8,128)S(1)}, u32[]{:S(2)}, u32[]{:S(2)}) collective-permute-start(f32[1,16,128,128]{3,2,1,0:T(8,128)S(1)} %get-tuple-element.23), channel_id=1, source_target_pairs={{0,1},{1,2},{2,3},{3,4},{4,5},{5,6},{6,7},{8,9},{9,10},{10,11},{11... | collective-permute-start | bytes 3145736 | tf_op jit(solution)/shard_map/ppermute | solution.py:16
  213.1 0.6 fusion.10
  213.7 0.3 fusion.12
  214.0 1.3 collective-permute-done.15
  215.3 0.8 pad_maximum_fusion
  216.1 0.6 fusion.1
  216.9 0.8 fusion.48
  217.7 56.4 %all-reduce.36.cloned.1.call-done = f32[2,128,128]{2,1,0:T(8,128)} async-done(((f32[2,128,128]{2,1,0:T(8,128)}), f32[2,128,128]{2,1,0:T(8,128)}) %all-reduce.36.cloned.1.call-update) | async-done | bytes 131088 | tf_op jit(solution)/shard_map/psum | solution.py:152
  274.0 1.6 copy.10
  (80 shorter events, 1.6 us)
Async XLA Ops:
  7.2 14.8 %copy-start = (f32[2,8,128,128]{3,2,1,0:T(8,128)S(1)}, f32[2,8,128,128]{3,2,1,0:T(8,128)}, u32[]{:S(2)}) copy-start(f32[2,8,128,128]{3,2,1,0:T(8,128)} %param.8) | copy-start | bytes 3145732
  7.2 266.9 %all-reduce.36.cloned.1.call-start = ((), (), s32[]{:S(2)}) async-start(), calls=%async_computation | async-start | bytes 262144 | tf_op jit(solution)/shard_map/psum | solution.py:152
  8.2 20.3 %collective-permute-start = (f32[1,128,128]{2,1,0:T(8,128)S(1)}, f32[1,128,128]{2,1,0:T(8,128)S(1)}, u32[]{:S(2)}, u32[]{:S(2)}) collective-permute-start(f32[1,128,128]{2,1,0:T(8,128)S(1)} %get-tuple-element.43), channel_id=1, source_target_pairs={{1,0},{2,1},{3,2},{4,3},{5,4},{6,5},{7,6},{9,8},{10,9},{11,10},{12... | collective-permute-start | bytes 196616 | tf_op jit(solution)/shard_map/ppermute | solution.py:19
  9.5 19.0 %collective-permute-start.1 = (f32[1,128,128]{2,1,0:T(8,128)S(1)}, f32[1,128,128]{2,1,0:T(8,128)S(1)}, u32[]{:S(2)}, u32[]{:S(2)}) collective-permute-start(f32[1,128,128]{2,1,0:T(8,128)S(1)} %get-tuple-element.42), channel_id=1, source_target_pairs={{0,1},{1,2},{2,3},{3,4},{4,5},{5,6},{6,7},{8,9},{9,10},{10,11},{11... | collective-permute-start | bytes 196616 | tf_op jit(solution)/shard_map/ppermute | solution.py:16
  14.6 12.1 %copy-start.15 = (f32[2,128,128]{2,1,0:T(8,128)S(1)}, f32[2,128,128]{2,1,0:T(8,128)}, u32[]{:S(2)}) copy-start(f32[2,128,128]{2,1,0:T(8,128)} %param.6) | copy-start | bytes 393220
  14.6 13.0 %copy-start.17 = (s32[8,4]{0,1:T(4,128)S(1)}, s32[8,4]{0,1:T(4,128)}, u32[]{:S(2)}) copy-start(s32[8,4]{0,1:T(4,128)} %param.10) | copy-start | bytes 388
  14.6 13.0 %copy-start.18 = (s32[128]{0:T(128)S(1)}, s32[128]{0:T(128)}, u32[]{:S(2)}) copy-start(s32[128]{0:T(128)} %param.9) | copy-start | bytes 1540
  14.6 13.3 %copy-start.1 = (f32[2,8,128,128]{3,2,1,0:T(8,128)S(1)}, f32[2,8,128,128]{3,2,1,0:T(8,128)}, u32[]{:S(2)}) copy-start(f32[2,8,128,128]{3,2,1,0:T(8,128)} %param.7) | copy-start | bytes 3145732
  14.6 14.1 %collective-permute-start.2 = (f32[1,8,128,128]{3,2,1,0:T(8,128)}, f32[1,8,128,128]{3,2,1,0:T(8,128)}, u32[]{:S(2)}, u32[]{:S(2)}) collective-permute-start(f32[1,8,128,128]{3,2,1,0:T(8,128)} %get-tuple-element.33), channel_id=1, source_target_pairs={{1,0},{2,1},{3,2},{4,3},{5,4},{6,5},{7,6},{9,8},{10,9},{11,10},{12... | collective-permute-start | bytes 1572872 | tf_op jit(solution)/shard_map/ppermute | solution.py:19
  16.1 12.7 %collective-permute-start.3 = (f32[1,8,128,128]{3,2,1,0:T(8,128)S(1)}, f32[1,8,128,128]{3,2,1,0:T(8,128)}, u32[]{:S(2)}, u32[]{:S(2)}) collective-permute-start(f32[1,8,128,128]{3,2,1,0:T(8,128)S(1)} %get-tuple-element.32), channel_id=1, source_target_pairs={{0,1},{1,2},{2,3},{3,4},{4,5},{5,6},{6,7},{8,9},{9,10},{10,11},{11... | collective-permute-start | bytes 1572872 | tf_op jit(solution)/shard_map/ppermute | solution.py:16
  23.1 71.4 %collective-permute-start.9 = (f32[1,8,128,128]{3,2,1,0:T(8,128)}, f32[1,8,128,128]{3,2,1,0:T(8,128)}, u32[]{:S(2)}, u32[]{:S(2)}) collective-permute-start(f32[1,8,128,128]{3,2,1,0:T(8,128)} %get-tuple-element.34), channel_id=1, source_target_pairs={{0,1},{1,2},{2,3},{3,4},{4,5},{5,6},{6,7},{8,9},{9,10},{10,11},{11... | collective-permute-start | bytes 1572872 | tf_op jit(solution)/shard_map/ppermute | solution.py:16
  26.8 1.7 copy-start.10
  26.9 1.7 copy-start.5
  28.7 1.4 copy-start.16
  30.9 35.5 %copy-start.3 = (f32[2,8,128,128]{3,2,1,0:T(8,128)}, f32[2,8,128,128]{3,2,1,0:T(8,128)S(1)}, u32[]{:S(2)}) copy-start(f32[2,8,128,128]{3,2,1,0:T(8,128)S(1)} %get-tuple-element.19) | copy-start | bytes 3145732
  31.0 4.9 %copy-start.11 = (f32[2,128,127]{2,1,0:T(8,128)S(1)}, f32[2,128,127]{2,1,0:T(8,128)}, u32[]{:S(2)}) copy-start(f32[2,128,127]{2,1,0:T(8,128)} %copy-done.10) | copy-start | bytes 390148
  31.0 5.3 %collective-permute-start.4 = (f32[1,8,128,128]{3,2,1,0:T(8,128)S(1)}, f32[1,8,128,128]{3,2,1,0:T(8,128)S(1)}, u32[]{:S(2)}, u32[]{:S(2)}) collective-permute-start(f32[1,8,128,128]{3,2,1,0:T(8,128)S(1)} %get-tuple-element.31), channel_id=1, source_target_pairs={{1,0},{2,1},{3,2},{4,3},{5,4},{6,5},{7,6},{9,8},{10,9},{11,10},{12... | collective-permute-start | bytes 1572872 | tf_op jit(solution)/shard_map/ppermute | solution.py:19
  32.5 3.7 %copy-start.6 = (f32[2,127,128]{2,1,0:T(8,128)S(1)}, f32[2,127,128]{2,1,0:T(8,128)}, u32[]{:S(2)}) copy-start(f32[2,127,128]{2,1,0:T(8,128)} %copy-done.5) | copy-start | bytes 390148
  32.5 4.8 %collective-permute-start.5 = (f32[1,8,128,128]{3,2,1,0:T(8,128)S(1)}, f32[1,8,128,128]{3,2,1,0:T(8,128)S(1)}, u32[]{:S(2)}, u32[]{:S(2)}) collective-permute-start(f32[1,8,128,128]{3,2,1,0:T(8,128)S(1)} %get-tuple-element.30), channel_id=1, source_target_pairs={{0,1},{1,2},{2,3},{3,4},{4,5},{5,6},{6,7},{8,9},{9,10},{10,11},{11... | collective-permute-start | bytes 1572872 | tf_op jit(solution)/shard_map/ppermute | solution.py:16
  68.0 26.5 %collective-permute-start.8 = (f32[1,8,128,128]{3,2,1,0:T(8,128)}, f32[1,8,128,128]{3,2,1,0:T(8,128)}, u32[]{:S(2)}, u32[]{:S(2)}) collective-permute-start(f32[1,8,128,128]{3,2,1,0:T(8,128)} %get-tuple-element.35), channel_id=1, source_target_pairs={{1,0},{2,1},{3,2},{4,3},{5,4},{6,5},{7,6},{9,8},{10,9},{11,10},{12... | collective-permute-start | bytes 1572872 | tf_op jit(solution)/shard_map/ppermute | solution.py:19
  87.0 4.6 %copy-start.12 = (f32[2,128,127]{2,1,0:T(8,128)S(1)}, f32[2,128,127]{2,1,0:T(8,128)}, u32[]{:S(2)}) copy-start(f32[2,128,127]{2,1,0:T(8,128)} %copy-done.10) | copy-start | bytes 390148
  87.1 7.4 %collective-permute-start.6 = (f32[1,8,128,128]{3,2,1,0:T(8,128)S(1)}, f32[1,8,128,128]{3,2,1,0:T(8,128)S(1)}, u32[]{:S(2)}, u32[]{:S(2)}) collective-permute-start(f32[1,8,128,128]{3,2,1,0:T(8,128)S(1)} %get-tuple-element.29), channel_id=1, source_target_pairs={{1,0},{2,1},{3,2},{4,3},{5,4},{6,5},{7,6},{9,8},{10,9},{11,10},{12... | collective-permute-start | bytes 1572872 | tf_op jit(solution)/shard_map/ppermute | solution.py:19
  88.4 4.8 %copy-start.7 = (f32[2,127,128]{2,1,0:T(8,128)S(1)}, f32[2,127,128]{2,1,0:T(8,128)}, u32[]{:S(2)}) copy-start(f32[2,127,128]{2,1,0:T(8,128)} %copy-done.5) | copy-start | bytes 390148
  88.4 6.1 %collective-permute-start.7 = (f32[1,8,128,128]{3,2,1,0:T(8,128)S(1)}, f32[1,8,128,128]{3,2,1,0:T(8,128)S(1)}, u32[]{:S(2)}, u32[]{:S(2)}) collective-permute-start(f32[1,8,128,128]{3,2,1,0:T(8,128)S(1)} %get-tuple-element.28), channel_id=1, source_target_pairs={{0,1},{1,2},{2,3},{3,4},{4,5},{5,6},{6,7},{8,9},{9,10},{10,11},{11... | collective-permute-start | bytes 1572872 | tf_op jit(solution)/shard_map/ppermute | solution.py:16
  118.6 15.3 %copy-start.19 = (f32[8]{0:T(128)S(1)}, f32[8]{0:T(128)}, u32[]{:S(2)}) copy-start(f32[8]{0:T(128)} %param.11) | copy-start | bytes 100
  133.9 3.8 %copy-start.20 = (f32[8]{0:T(128)}, f32[8]{0:T(128)S(1)}, u32[]{:S(2)}) copy-start(f32[8]{0:T(128)S(1)} %psum.74) | copy-start | bytes 100
  137.6 4.6 %copy-start.13 = (f32[2,128,127]{2,1,0:T(8,128)S(1)}, f32[2,128,127]{2,1,0:T(8,128)}, u32[]{:S(2)}) copy-start(f32[2,128,127]{2,1,0:T(8,128)} %copy-done.10) | copy-start | bytes 390148
  137.7 5.0 %collective-permute-start.10 = (f32[1,8,128,128]{3,2,1,0:T(8,128)S(1)}, f32[1,8,128,128]{3,2,1,0:T(8,128)S(1)}, u32[]{:S(2)}, u32[]{:S(2)}) collective-permute-start(f32[1,8,128,128]{3,2,1,0:T(8,128)S(1)} %get-tuple-element.27), channel_id=1, source_target_pairs={{1,0},{2,1},{3,2},{4,3},{5,4},{6,5},{7,6},{9,8},{10,9},{11,10},{12... | collective-permute-start | bytes 1572872 | tf_op jit(solution)/shard_map/ppermute | solution.py:19
  139.0 3.6 %copy-start.8 = (f32[2,127,128]{2,1,0:T(8,128)S(1)}, f32[2,127,128]{2,1,0:T(8,128)}, u32[]{:S(2)}) copy-start(f32[2,127,128]{2,1,0:T(8,128)} %copy-done.5) | copy-start | bytes 390148
  139.0 4.7 %collective-permute-start.11 = (f32[1,8,128,128]{3,2,1,0:T(8,128)S(1)}, f32[1,8,128,128]{3,2,1,0:T(8,128)S(1)}, u32[]{:S(2)}, u32[]{:S(2)}) collective-permute-start(f32[1,8,128,128]{3,2,1,0:T(8,128)S(1)} %get-tuple-element.26), channel_id=1, source_target_pairs={{0,1},{1,2},{2,3},{3,4},{4,5},{5,6},{6,7},{8,9},{9,10},{10,11},{11... | collective-permute-start | bytes 1572872 | tf_op jit(solution)/shard_map/ppermute | solution.py:16
  144.7 33.3 %copy-start.4 = (f32[2,8,128,128]{3,2,1,0:T(8,128)}, f32[2,8,128,128]{3,2,1,0:T(8,128)S(1)}, u32[]{:S(2)}) copy-start(f32[2,8,128,128]{3,2,1,0:T(8,128)S(1)} %get-tuple-element.12) | copy-start | bytes 3145732
  179.5 4.6 %copy-start.14 = (f32[2,128,127]{2,1,0:T(8,128)S(1)}, f32[2,128,127]{2,1,0:T(8,128)}, u32[]{:S(2)}) copy-start(f32[2,128,127]{2,1,0:T(8,128)} %copy-done.10) | copy-start | bytes 390148
  179.6 5.0 %collective-permute-start.12 = (f32[1,8,128,128]{3,2,1,0:T(8,128)S(1)}, f32[1,8,128,128]{3,2,1,0:T(8,128)S(1)}, u32[]{:S(2)}, u32[]{:S(2)}) collective-permute-start(f32[1,8,128,128]{3,2,1,0:T(8,128)S(1)} %get-tuple-element.25), channel_id=1, source_target_pairs={{1,0},{2,1},{3,2},{4,3},{5,4},{6,5},{7,6},{9,8},{10,9},{11,10},{12... | collective-permute-start | bytes 1572872 | tf_op jit(solution)/shard_map/ppermute | solution.py:19
  180.9 3.6 %copy-start.9 = (f32[2,127,128]{2,1,0:T(8,128)S(1)}, f32[2,127,128]{2,1,0:T(8,128)}, u32[]{:S(2)}) copy-start(f32[2,127,128]{2,1,0:T(8,128)} %copy-done.5) | copy-start | bytes 390148
  180.9 4.7 %collective-permute-start.13 = (f32[1,8,128,128]{3,2,1,0:T(8,128)S(1)}, f32[1,8,128,128]{3,2,1,0:T(8,128)S(1)}, u32[]{:S(2)}, u32[]{:S(2)}) collective-permute-start(f32[1,8,128,128]{3,2,1,0:T(8,128)S(1)} %get-tuple-element.24), channel_id=1, source_target_pairs={{0,1},{1,2},{2,3},{3,4},{4,5},{5,6},{6,7},{8,9},{9,10},{10,11},{11... | collective-permute-start | bytes 1572872 | tf_op jit(solution)/shard_map/ppermute | solution.py:16
  207.2 1.2 copy-start.2
  208.7 5.3 %collective-permute-start.14 = (f32[1,16,128,128]{3,2,1,0:T(8,128)S(1)}, f32[1,16,128,128]{3,2,1,0:T(8,128)S(1)}, u32[]{:S(2)}, u32[]{:S(2)}) collective-permute-start(f32[1,16,128,128]{3,2,1,0:T(8,128)S(1)} %get-tuple-element.22), channel_id=1, source_target_pairs={{1,0},{2,1},{3,2},{4,3},{5,4},{6,5},{7,6},{9,8},{10,9},{11,10},{12... | collective-permute-start | bytes 3145736 | tf_op jit(solution)/shard_map/ppermute | solution.py:19
  210.0 5.3 %collective-permute-start.15 = (f32[1,16,128,128]{3,2,1,0:T(8,128)S(1)}, f32[1,16,128,128]{3,2,1,0:T(8,128)S(1)}, u32[]{:S(2)}, u32[]{:S(2)}) collective-permute-start(f32[1,16,128,128]{3,2,1,0:T(8,128)S(1)} %get-tuple-element.23), channel_id=1, source_target_pairs={{0,1},{1,2},{2,3},{3,4},{4,5},{5,6},{6,7},{8,9},{9,10},{10,11},{11... | collective-permute-start | bytes 3145736 | tf_op jit(solution)/shard_map/ppermute | solution.py:16
Sparse Core Ops, SparseCore 0:
  217.8 56.2 all-reduce.35
where the time goes:
time: 283 us; the launch traced here: 282 us
  blocking collectives  130 us (46%)
  waiting for transfers between devices  60.6 us (21%)
  starting transfers between devices  39.3 us (14%)
  other arithmetic  31.2 us (11%)
  between operations  14.7 us (5%)
  local copies, waits for them, and re-layouts  7.01 us (2%)
    psum x6, blocking collectives, pattern_sum(): return lax.psum(local_terms, 'vox')  117 us
    psum x1, waiting for transfers between devices, per_device(): gradient = lax.psum(local_gradient, 'pat')  56.4 us
    ppermute x8, starting transfers between devices, extended(): lax.ppermute(lax.slice_in_dim(block, block.shape[dim] - width, None, axis...  28.6 us
    psum x1, blocking collectives, per_device(): predicted = lax.psum(inner(probe_weights, forward), 'vox')  12.4 us
    ppermute x8, starting transfers between devices, extended(): lax.ppermute(lax.slice_in_dim(block, 0, width, axis=dim), axis, backward)  10.6 us
    reduce_sum x7, other arithmetic, inner(): return jnp.sum(left_factor * right_factor, axis=(0, 2, 3))  8.68 us
  transfers between devices with their start and end apart: 17, of which 5 were waited for; matrix products, arithmetic and copies ran while one was open for 6% of the time, Pallas kernels for 0%

commit v1 on v0

--- a/solution.py
+++ b/solution.py
@@ -149,7 +149,7 @@
     local_gradient = -0.5 * (
         grad_depth + both_sides(row_products, 1) + both_sides(column_products, 2)
     )
-    gradient = lax.psum(local_gradient, "pat")
+    gradient = jnp.sum(lax.all_gather(local_gradient, "pat"), axis=0)
     return (gradient, predicted)
 
 

time: 283 us -> 248 us (0.88)
  the two profiles are of different devices: /device:TPU:0 before, /device:TPU:4 now
where the time goes in v1:
time: 248 us; the launch traced here: 247 us
  blocking collectives  105 us (42%)
  waiting for transfers between devices  64.9 us (26%)
  starting transfers between devices  38.7 us (16%)
  other arithmetic  31.2 us (13%)
  local copies, waits for them, and re-layouts  5.45 us (2%)
    psum x6, blocking collectives, pattern_sum(): return lax.psum(local_terms, 'vox')  77.5 us
    ppermute x8, waiting for transfers between devices, extended(): lax.ppermute(lax.slice_in_dim(block, 0, width, axis=dim), axis, backward)  47.7 us
    ppermute x8, starting transfers between devices, extended(): lax.ppermute(lax.slice_in_dim(block, 0, width, axis=dim), axis, backward)  21.1 us
    ppermute x8, starting transfers between devices, extended(): lax.ppermute(lax.slice_in_dim(block, block.shape[dim] - width, None, axis...  17.6 us
    ppermute x8, waiting for transfers between devices, extended(): lax.ppermute(lax.slice_in_dim(block, block.shape[dim] - width, None, axis...  17.1 us
    all_gather x1, blocking collectives, per_device(): gradient = jnp.sum(lax.all_gather(local_gradient, 'pat'), axis=0)  15.9 us
    psum x1, blocking collectives, per_device(): predicted = lax.psum(inner(probe_weights, forward), 'vox')  11.8 us
    reduce_sum x7, other arithmetic, inner(): return jnp.sum(left_factor * right_factor, axis=(0, 2, 3))  8.69 us
  transfers between devices with their start and end apart: 16, of which 12 were waited for; matrix products, arithmetic and copies ran while one was open for 7% of the time, Pallas kernels for 0%

profile of v1, /device:TPU:4, one launch (start us, length us, event | category | flops | bytes accessed | tf_op | source)
XLA Modules:
  0.0 246.7 jit_solution(10584825285196675312)
XLA Ops:
  0.6 1.0 fusion.63
  1.6 2.8 %collective-permute-start = (f32[1,128,128]{2,1,0:T(8,128)S(1)}, f32[1,128,128]{2,1,0:T(8,128)S(1)}, u32[]{:S(2)}, u32[]{:S(2)}) collective-permute-start(f32[1,128,128]{2,1,0:T(8,128)S(1)} %get-tuple-element.43), channel_id=1, source_target_pairs={{1,0},{2,1},{3,2},{4,3},{5,4},{6,5},{7,6},{9,8},{10,9},{11,10},{12... | collective-permute-start | bytes 196616 | tf_op jit(solution)/shard_map/ppermute | solution.py:19
  4.4 1.9 collective-permute-start.1
  6.3 2.1 fusion.61
  8.4 4.7 %collective-permute-start.2 = (f32[1,8,128,128]{3,2,1,0:T(8,128)}, f32[1,8,128,128]{3,2,1,0:T(8,128)}, u32[]{:S(2)}, u32[]{:S(2)}) collective-permute-start(f32[1,8,128,128]{3,2,1,0:T(8,128)} %get-tuple-element.33), channel_id=1, source_target_pairs={{1,0},{2,1},{3,2},{4,3},{5,4},{6,5},{7,6},{9,8},{10,9},{11,10},{12... | collective-permute-start | bytes 1572872 | tf_op jit(solution)/shard_map/ppermute | solution.py:19
  13.1 1.9 collective-permute-start.3
  15.0 1.1 fusion.62
  16.1 1.9 collective-permute-start.9
  18.2 0.7 iota_add_fusion
  19.2 0.3 subtract_multiply_fusion.2
  20.0 4.8 %collective-permute-done.2 = f32[1,8,128,128]{3,2,1,0:T(8,128)} collective-permute-done((f32[1,8,128,128]{3,2,1,0:T(8,128)}, f32[1,8,128,128]{3,2,1,0:T(8,128)}, u32[]{:S(2)}, u32[]{:S(2)}) %collective-permute-start.2) | collective-permute-done | bytes 524320 | tf_op jit(solution)/shard_map/ppermute | solution.py:19
  24.9 1.0 collective-permute-done.3
  25.8 1.3 fusion.2
  27.2 0.8 broadcast_divide_fusion.1
  28.1 3.9 %collective-permute-start.4 = (f32[1,8,128,128]{3,2,1,0:T(8,128)S(1)}, f32[1,8,128,128]{3,2,1,0:T(8,128)S(1)}, u32[]{:S(2)}, u32[]{:S(2)}) collective-permute-start(f32[1,8,128,128]{3,2,1,0:T(8,128)S(1)} %get-tuple-element.31), channel_id=1, source_target_pairs={{1,0},{2,1},{3,2},{4,3},{5,4},{6,5},{7,6},{9,8},{10,9},{11,10},{12... | collective-permute-start | bytes 1572872 | tf_op jit(solution)/shard_map/ppermute | solution.py:19
  32.0 2.1 collective-permute-start.5
  34.1 0.3 fusion.36
  34.6 7.7 %collective-permute-done.4 = f32[1,8,128,128]{3,2,1,0:T(8,128)S(1)} collective-permute-done((f32[1,8,128,128]{3,2,1,0:T(8,128)S(1)}, f32[1,8,128,128]{3,2,1,0:T(8,128)S(1)}, u32[]{:S(2)}, u32[]{:S(2)}) %collective-permute-start.4) | collective-permute-done | bytes 524320 | tf_op jit(solution)/shard_map/ppermute | solution.py:19
  42.3 1.3 collective-permute-done.5
  43.7 1.7 multiply_reduce_fusion.5
  45.4 13.3 %all-reduce.33 = (f32[8]{0:T(128)S(1)}, f32[8]{0:T(128)S(1)}) all-reduce(f32[8]{0:T(128)S(1)} %get-tuple-element.5, f32[8]{0:T(128)S(1)} %get-tuple-element.4), channel_id=1, replica_groups=mesh['pat'=4,'vox'=8] {'vox'}, use_global_device_ids=true, to_apply=%region_2.3 | all-reduce | flops 16 | bytes 128 | tf_op jit(solution)/shard_map/psum | solution.py:61
  58.7 1.6 multiply_reduce_fusion.4
  60.3 1.9 collective-permute-start.8
  62.2 16.4 %psum.65 = f32[8]{0:T(128)S(1)} all-reduce(f32[8]{0:T(128)S(1)} %multiply_reduce_fusion.4), channel_id=1, replica_groups=mesh['pat'=4,'vox'=8] {'vox'}, use_global_device_ids=true, to_apply=%region_6.7 | all-reduce | flops 8 | bytes 64 | tf_op jit(solution)/shard_map/psum | solution.py:61
  78.7 1.8 multiply_add_fusion.3
  80.6 1.9 collective-permute-start.6
  82.5 2.5 %collective-permute-start.7 = (f32[1,8,128,128]{3,2,1,0:T(8,128)S(1)}, f32[1,8,128,128]{3,2,1,0:T(8,128)S(1)}, u32[]{:S(2)}, u32[]{:S(2)}) collective-permute-start(f32[1,8,128,128]{3,2,1,0:T(8,128)S(1)} %get-tuple-element.28), channel_id=1, source_target_pairs={{0,1},{1,2},{2,3},{3,4},{4,5},{5,6},{6,7},{8,9},{9,10},{10,11},{11... | collective-permute-start | bytes 1572872 | tf_op jit(solution)/shard_map/ppermute | solution.py:16
  85.1 1.6 fusion.29
  86.7 1.3 fusion.30
  87.9 5.0 %collective-permute-done.6 = f32[1,8,128,128]{3,2,1,0:T(8,128)S(1)} collective-permute-done((f32[1,8,128,128]{3,2,1,0:T(8,128)S(1)}, f32[1,8,128,128]{3,2,1,0:T(8,128)S(1)}, u32[]{:S(2)}, u32[]{:S(2)}) %collective-permute-start.6) | collective-permute-done | bytes 524320 | tf_op jit(solution)/shard_map/ppermute | solution.py:19
  92.9 2.1 collective-permute-done.7
  95.0 2.8 %fusion.4 = (f32[3,8,128,128]{3,2,1,0:T(8,128)S(1)}, f32[3,8,128,128]{3,2,1,0:T(8,128)}) fusion(f32[1,8,128,128]{3,2,1,0:T(8,128)S(1)} %collective-permute-done.6, f32[2,8,128,128]{3,2,1,0:T(8,128)S(1)} %multiply_add_fusion.3, f32[1,8,128,128]{3,2,1,0:T(8,128)S(1)} %collective-permute-done.7, f32[3,128,128]{2,1,0:T(8,128)S(1)} %fusion.45, ...), kind=kLoop, calls=%fused_computation.13 | loop fusion | flops 3145728 | bytes 7536640 | tf_op jit(solution)/shard_map/mul | solution.py:43
  97.8 0.7 fusion.35
  98.5 12.5 %psum.66 = f32[8]{0:T(128)S(1)} all-reduce(f32[8]{0:T(128)S(1)} %fusion.35), channel_id=1, replica_groups=mesh['pat'=4,'vox'=8] {'vox'}, use_global_device_ids=true, to_apply=%region_8.9 | all-reduce | flops 8 | bytes 64 | tf_op jit(solution)/shard_map/psum | solution.py:61
  111.0 2.8 %multiply_reduce_fusion.3 = (f32[8]{0:T(128)S(1)}, f32[2,8,128,128]{3,2,1,0:T(8,128)}) fusion(s32[2,128,128]{2,1,0:T(8,128)} %iota_add_fusion, s32[8]{0:T(128)S(1)} %get-tuple-element.45, s32[8]{0:T(128)S(1)} %get-tuple-element.46, f32[2,8,128,128]{3,2,1,0:T(8,128)S(1)} %multiply_add_fusion.3, f32[8]{0:T(128)S(1)} %div.49, ...), kind=kLoop, calls=%fused_computation.84 | loop fusion | flops 3145720 | bytes 4456608 | tf_op jit(solution)/shard_map/reduce_sum | solution.py:53
  113.8 11.8 %psum.67 = f32[8]{0:T(128)S(1)} all-reduce(f32[8]{0:T(128)S(1)} %get-tuple-element.15), channel_id=1, replica_groups=mesh['pat'=4,'vox'=8] {'vox'}, use_global_device_ids=true, to_apply=%region_10.11 | all-reduce | flops 8 | bytes 64 | tf_op jit(solution)/shard_map/psum | solution.py:126
  125.6 3.7 %broadcast_divide_fusion = (f32[2,8,128,128]{3,2,1,0:T(8,128)S(1)}, f32[2,8,128,128]{3,2,1,0:T(8,128)S(1)}) fusion(f32[2,128,128]{2,1,0:T(8,128)S(1)} %fusion.51, f32[2,8,128,127]{3,2,1,0:T(8,128)} %get-tuple-element.41, f32[2,8,127,128]{3,2,1,0:T(8,128)} %get-tuple-element.39, f32[3,8,128,128]{3,2,1,0:T(8,128)} %get-tuple-element.37, ...), kind=kLoop, calls=%fused_computation.94 | loop fusion | flops 3932160 | bytes 7585888 | tf_op jit(solution)/shard_map/div | solution.py:67
  129.5 1.9 collective-permute-start.10
  131.4 2.5 %collective-permute-start.11 = (f32[1,8,128,128]{3,2,1,0:T(8,128)S(1)}, f32[1,8,128,128]{3,2,1,0:T(8,128)S(1)}, u32[]{:S(2)}, u32[]{:S(2)}) collective-permute-start(f32[1,8,128,128]{3,2,1,0:T(8,128)S(1)} %get-tuple-element.26), channel_id=1, source_target_pairs={{0,1},{1,2},{2,3},{3,4},{4,5},{5,6},{6,7},{8,9},{9,10},{10,11},{11... | collective-permute-start | bytes 1572872 | tf_op jit(solution)/shard_map/ppermute | solution.py:16
  134.0 0.3 fusion.20
  134.5 6.2 %collective-permute-done.10 = f32[1,8,128,128]{3,2,1,0:T(8,128)S(1)} collective-permute-done((f32[1,8,128,128]{3,2,1,0:T(8,128)S(1)}, f32[1,8,128,128]{3,2,1,0:T(8,128)S(1)}, u32[]{:S(2)}, u32[]{:S(2)}) %collective-permute-start.10) | collective-permute-done | bytes 524320 | tf_op jit(solution)/shard_map/ppermute | solution.py:19
  140.7 4.4 %collective-permute-done.11 = f32[1,8,128,128]{3,2,1,0:T(8,128)S(1)} collective-permute-done((f32[1,8,128,128]{3,2,1,0:T(8,128)S(1)}, f32[1,8,128,128]{3,2,1,0:T(8,128)S(1)}, u32[]{:S(2)}, u32[]{:S(2)}) %collective-permute-start.11) | collective-permute-done | bytes 524320 | tf_op jit(solution)/shard_map/ppermute | solution.py:16
  145.3 0.8 multiply_reduce_fusion.1
  146.1 11.8 %all-reduce.32 = (f32[8]{0:T(128)S(1)}, f32[8]{0:T(128)S(1)}) all-reduce(f32[8]{0:T(128)S(1)} %get-tuple-element.3, f32[8]{0:T(128)S(1)} %get-tuple-element.2), channel_id=1, replica_groups=mesh['pat'=4,'vox'=8] {'vox'}, use_global_device_ids=true, to_apply=%region_12.13 | all-reduce | flops 16 | bytes 128 | tf_op jit(solution)/shard_map/psum | solution.py:61
  157.9 0.3 multiply_reduce_fusion
  158.3 11.8 %psum.70 = f32[8]{0:T(128)S(1)} all-reduce(f32[8]{0:T(128)S(1)} %multiply_reduce_fusion), channel_id=1, replica_groups=mesh['pat'=4,'vox'=8] {'vox'}, use_global_device_ids=true, to_apply=%region_16.17 | all-reduce | flops 8 | bytes 64 | tf_op jit(solution)/shard_map/psum | solution.py:61
  170.1 1.5 multiply_add_fusion.1
  171.7 2.1 collective-permute-start.12
  173.8 2.4 collective-permute-start.13
  176.2 0.3 fusion.13
  176.7 6.6 %collective-permute-done.12 = f32[1,8,128,128]{3,2,1,0:T(8,128)S(1)} collective-permute-done((f32[1,8,128,128]{3,2,1,0:T(8,128)S(1)}, f32[1,8,128,128]{3,2,1,0:T(8,128)S(1)}, u32[]{:S(2)}, u32[]{:S(2)}) %collective-permute-start.12) | collective-permute-done | bytes 524320 | tf_op jit(solution)/shard_map/ppermute | solution.py:19
  183.3 3.5 %collective-permute-done.13 = f32[1,8,128,128]{3,2,1,0:T(8,128)S(1)} collective-permute-done((f32[1,8,128,128]{3,2,1,0:T(8,128)S(1)}, f32[1,8,128,128]{3,2,1,0:T(8,128)S(1)}, u32[]{:S(2)}, u32[]{:S(2)}) %collective-permute-start.13) | collective-permute-done | bytes 524320 | tf_op jit(solution)/shard_map/ppermute | solution.py:16
  187.0 0.7 fusion.19
  187.7 11.8 %psum.71 = f32[8]{0:T(128)S(1)} all-reduce(f32[8]{0:T(128)S(1)} %fusion.19), channel_id=1, replica_groups=mesh['pat'=4,'vox'=8] {'vox'}, use_global_device_ids=true, to_apply=%region_18.19 | all-reduce | flops 8 | bytes 64 | tf_op jit(solution)/shard_map/psum | solution.py:61
  199.8 0.9 copy-done.2
  201.0 1.9 collective-permute-start.14
  202.9 2.4 collective-permute-start.15
  205.3 0.6 fusion.10
  206.2 17.4 %collective-permute-done.14 = f32[1,16,128,128]{3,2,1,0:T(8,128)S(1)} collective-permute-done((f32[1,16,128,128]{3,2,1,0:T(8,128)S(1)}, f32[1,16,128,128]{3,2,1,0:T(8,128)S(1)}, u32[]{:S(2)}, u32[]{:S(2)}) %collective-permute-start.14) | collective-permute-done | bytes 1048608 | tf_op jit(solution)/shard_map/ppermute | solution.py:19
  223.6 4.9 %collective-permute-done.15 = f32[1,16,128,128]{3,2,1,0:T(8,128)S(1)} collective-permute-done((f32[1,16,128,128]{3,2,1,0:T(8,128)S(1)}, f32[1,16,128,128]{3,2,1,0:T(8,128)S(1)}, u32[]{:S(2)}, u32[]{:S(2)}) %collective-permute-start.15) | collective-permute-done | bytes 1048608 | tf_op jit(solution)/shard_map/ppermute | solution.py:16
  228.5 0.8 pad_maximum_fusion
  229.3 0.6 fusion.1
  230.2 15.9 %all-gather = f32[8,128,128]{2,1,0:T(8,128)S(1)} all-gather(f32[2,128,128]{2,1,0:T(8,128)S(1)} %fusion.48), channel_id=2, replica_groups=mesh['pat'=4,'vox'=8] {'pat'}, dimensions={0}, use_global_device_ids=true | all-gather | bytes 655360 | tf_op jit(solution)/shard_map/all_gather | solution.py:152
  246.0 0.7 reduce_sum.139
  (78 shorter events, 3.2 us)
Async XLA Ops:
  0.6 14.4 %copy-start = (f32[2,8,128,128]{3,2,1,0:T(8,128)S(1)}, f32[2,8,128,128]{3,2,1,0:T(8,128)}, u32[]{:S(2)}) copy-start(f32[2,8,128,128]{3,2,1,0:T(8,128)} %param.8) | copy-start | bytes 3145732
  1.6 18.2 %collective-permute-start = (f32[1,128,128]{2,1,0:T(8,128)S(1)}, f32[1,128,128]{2,1,0:T(8,128)S(1)}, u32[]{:S(2)}, u32[]{:S(2)}) collective-permute-start(f32[1,128,128]{2,1,0:T(8,128)S(1)} %get-tuple-element.43), channel_id=1, source_target_pairs={{1,0},{2,1},{3,2},{4,3},{5,4},{6,5},{7,6},{9,8},{10,9},{11,10},{12... | collective-permute-start | bytes 196616 | tf_op jit(solution)/shard_map/ppermute | solution.py:19
  4.4 15.4 %collective-permute-start.1 = (f32[1,128,128]{2,1,0:T(8,128)S(1)}, f32[1,128,128]{2,1,0:T(8,128)S(1)}, u32[]{:S(2)}, u32[]{:S(2)}) collective-permute-start(f32[1,128,128]{2,1,0:T(8,128)S(1)} %get-tuple-element.42), channel_id=1, source_target_pairs={{0,1},{1,2},{2,3},{3,4},{4,5},{5,6},{6,7},{8,9},{9,10},{10,11},{11... | collective-permute-start | bytes 196616 | tf_op jit(solution)/shard_map/ppermute | solution.py:16
  8.4 9.6 %copy-start.15 = (f32[2,128,128]{2,1,0:T(8,128)S(1)}, f32[2,128,128]{2,1,0:T(8,128)}, u32[]{:S(2)}) copy-start(f32[2,128,128]{2,1,0:T(8,128)} %param.6) | copy-start | bytes 393220
  8.4 10.5 %copy-start.17 = (s32[8,4]{0,1:T(4,128)S(1)}, s32[8,4]{0,1:T(4,128)}, u32[]{:S(2)}) copy-start(s32[8,4]{0,1:T(4,128)} %param.10) | copy-start | bytes 388
  8.4 10.5 %copy-start.18 = (s32[128]{0:T(128)S(1)}, s32[128]{0:T(128)}, u32[]{:S(2)}) copy-start(s32[128]{0:T(128)} %param.9) | copy-start | bytes 1540
  8.4 10.8 %copy-start.1 = (f32[2,8,128,128]{3,2,1,0:T(8,128)S(1)}, f32[2,8,128,128]{3,2,1,0:T(8,128)}, u32[]{:S(2)}) copy-start(f32[2,8,128,128]{3,2,1,0:T(8,128)} %param.7) | copy-start | bytes 3145732
  8.4 16.4 %collective-permute-start.2 = (f32[1,8,128,128]{3,2,1,0:T(8,128)}, f32[1,8,128,128]{3,2,1,0:T(8,128)}, u32[]{:S(2)}, u32[]{:S(2)}) collective-permute-start(f32[1,8,128,128]{3,2,1,0:T(8,128)} %get-tuple-element.33), channel_id=1, source_target_pairs={{1,0},{2,1},{3,2},{4,3},{5,4},{6,5},{7,6},{9,8},{10,9},{11,10},{12... | collective-permute-start | bytes 1572872 | tf_op jit(solution)/shard_map/ppermute | solution.py:19
  13.1 12.7 %collective-permute-start.3 = (f32[1,8,128,128]{3,2,1,0:T(8,128)S(1)}, f32[1,8,128,128]{3,2,1,0:T(8,128)}, u32[]{:S(2)}, u32[]{:S(2)}) collective-permute-start(f32[1,8,128,128]{3,2,1,0:T(8,128)S(1)} %get-tuple-element.32), channel_id=1, source_target_pairs={{0,1},{1,2},{2,3},{3,4},{4,5},{5,6},{6,7},{8,9},{9,10},{10,11},{11... | collective-permute-start | bytes 1572872 | tf_op jit(solution)/shard_map/ppermute | solution.py:16
  16.1 71.8 %collective-permute-start.9 = (f32[1,8,128,128]{3,2,1,0:T(8,128)}, f32[1,8,128,128]{3,2,1,0:T(8,128)}, u32[]{:S(2)}, u32[]{:S(2)}) collective-permute-start(f32[1,8,128,128]{3,2,1,0:T(8,128)} %get-tuple-element.34), channel_id=1, source_target_pairs={{0,1},{1,2},{2,3},{3,4},{4,5},{5,6},{6,7},{8,9},{9,10},{10,11},{11... | collective-permute-start | bytes 1572872 | tf_op jit(solution)/shard_map/ppermute | solution.py:16
  18.2 1.7 copy-start.10
  18.2 1.7 copy-start.5
  20.0 7.2 %copy-start.16 = (s32[2,128,128]{2,1,0:T(8,128)S(1)}, s32[2,128,128]{2,1,0:T(8,128)}, u32[]{:S(2)}) copy-start(s32[2,128,128]{2,1,0:T(8,128)} %iota_add_fusion) | copy-start | bytes 393220
  28.0 30.7 %copy-start.3 = (f32[2,8,128,128]{3,2,1,0:T(8,128)}, f32[2,8,128,128]{3,2,1,0:T(8,128)S(1)}, u32[]{:S(2)}) copy-start(f32[2,8,128,128]{3,2,1,0:T(8,128)S(1)} %get-tuple-element.19) | copy-start | bytes 3145732
  28.0 6.0 %copy-start.11 = (f32[2,128,127]{2,1,0:T(8,128)S(1)}, f32[2,128,127]{2,1,0:T(8,128)}, u32[]{:S(2)}) copy-start(f32[2,128,127]{2,1,0:T(8,128)} %copy-done.10) | copy-start | bytes 390148
  28.1 14.1 %collective-permute-start.4 = (f32[1,8,128,128]{3,2,1,0:T(8,128)S(1)}, f32[1,8,128,128]{3,2,1,0:T(8,128)S(1)}, u32[]{:S(2)}, u32[]{:S(2)}) collective-permute-start(f32[1,8,128,128]{3,2,1,0:T(8,128)S(1)} %get-tuple-element.31), channel_id=1, source_target_pairs={{1,0},{2,1},{3,2},{4,3},{5,4},{6,5},{7,6},{9,8},{10,9},{11,10},{12... | collective-permute-start | bytes 1572872 | tf_op jit(solution)/shard_map/ppermute | solution.py:19
  32.0 2.4 copy-start.6
  32.0 11.5 %collective-permute-start.5 = (f32[1,8,128,128]{3,2,1,0:T(8,128)S(1)}, f32[1,8,128,128]{3,2,1,0:T(8,128)S(1)}, u32[]{:S(2)}, u32[]{:S(2)}) collective-permute-start(f32[1,8,128,128]{3,2,1,0:T(8,128)S(1)} %get-tuple-element.30), channel_id=1, source_target_pairs={{0,1},{1,2},{2,3},{3,4},{4,5},{5,6},{6,7},{8,9},{9,10},{10,11},{11... | collective-permute-start | bytes 1572872 | tf_op jit(solution)/shard_map/ppermute | solution.py:16
  60.3 27.6 %collective-permute-start.8 = (f32[1,8,128,128]{3,2,1,0:T(8,128)}, f32[1,8,128,128]{3,2,1,0:T(8,128)}, u32[]{:S(2)}, u32[]{:S(2)}) collective-permute-start(f32[1,8,128,128]{3,2,1,0:T(8,128)} %get-tuple-element.35), channel_id=1, source_target_pairs={{1,0},{2,1},{3,2},{4,3},{5,4},{6,5},{7,6},{9,8},{10,9},{11,10},{12... | collective-permute-start | bytes 1572872 | tf_op jit(solution)/shard_map/ppermute | solution.py:19
  80.5 4.6 %copy-start.12 = (f32[2,128,127]{2,1,0:T(8,128)S(1)}, f32[2,128,127]{2,1,0:T(8,128)}, u32[]{:S(2)}) copy-start(f32[2,128,127]{2,1,0:T(8,128)} %copy-done.10) | copy-start | bytes 390148
  80.6 12.3 %collective-permute-start.6 = (f32[1,8,128,128]{3,2,1,0:T(8,128)S(1)}, f32[1,8,128,128]{3,2,1,0:T(8,128)S(1)}, u32[]{:S(2)}, u32[]{:S(2)}) collective-permute-start(f32[1,8,128,128]{3,2,1,0:T(8,128)S(1)} %get-tuple-element.29), channel_id=1, source_target_pairs={{1,0},{2,1},{3,2},{4,3},{5,4},{6,5},{7,6},{9,8},{10,9},{11,10},{12... | collective-permute-start | bytes 1572872 | tf_op jit(solution)/shard_map/ppermute | solution.py:19
  82.5 4.2 %copy-start.7 = (f32[2,127,128]{2,1,0:T(8,128)S(1)}, f32[2,127,128]{2,1,0:T(8,128)}, u32[]{:S(2)}) copy-start(f32[2,127,128]{2,1,0:T(8,128)} %copy-done.5) | copy-start | bytes 390148
  82.5 12.5 %collective-permute-start.7 = (f32[1,8,128,128]{3,2,1,0:T(8,128)S(1)}, f32[1,8,128,128]{3,2,1,0:T(8,128)S(1)}, u32[]{:S(2)}, u32[]{:S(2)}) collective-permute-start(f32[1,8,128,128]{3,2,1,0:T(8,128)S(1)} %get-tuple-element.28), channel_id=1, source_target_pairs={{0,1},{1,2},{2,3},{3,4},{4,5},{5,6},{6,7},{8,9},{9,10},{10,11},{11... | collective-permute-start | bytes 1572872 | tf_op jit(solution)/shard_map/ppermute | solution.py:16
  111.0 14.6 %copy-start.19 = (f32[8]{0:T(128)S(1)}, f32[8]{0:T(128)}, u32[]{:S(2)}) copy-start(f32[8]{0:T(128)} %param.11) | copy-start | bytes 100
  125.6 3.8 %copy-start.20 = (f32[8]{0:T(128)}, f32[8]{0:T(128)S(1)}, u32[]{:S(2)}) copy-start(f32[8]{0:T(128)S(1)} %psum.67) | copy-start | bytes 100
  129.4 4.6 %copy-start.13 = (f32[2,128,127]{2,1,0:T(8,128)S(1)}, f32[2,128,127]{2,1,0:T(8,128)}, u32[]{:S(2)}) copy-start(f32[2,128,127]{2,1,0:T(8,128)} %copy-done.10) | copy-start | bytes 390148
  129.5 11.3 %collective-permute-start.10 = (f32[1,8,128,128]{3,2,1,0:T(8,128)S(1)}, f32[1,8,128,128]{3,2,1,0:T(8,128)S(1)}, u32[]{:S(2)}, u32[]{:S(2)}) collective-permute-start(f32[1,8,128,128]{3,2,1,0:T(8,128)S(1)} %get-tuple-element.27), channel_id=1, source_target_pairs={{1,0},{2,1},{3,2},{4,3},{5,4},{6,5},{7,6},{9,8},{10,9},{11,10},{12... | collective-permute-start | bytes 1572872 | tf_op jit(solution)/shard_map/ppermute | solution.py:19
  131.4 2.9 %copy-start.8 = (f32[2,127,128]{2,1,0:T(8,128)S(1)}, f32[2,127,128]{2,1,0:T(8,128)}, u32[]{:S(2)}) copy-start(f32[2,127,128]{2,1,0:T(8,128)} %copy-done.5) | copy-start | bytes 390148
  131.4 13.7 %collective-permute-start.11 = (f32[1,8,128,128]{3,2,1,0:T(8,128)S(1)}, f32[1,8,128,128]{3,2,1,0:T(8,128)S(1)}, u32[]{:S(2)}, u32[]{:S(2)}) collective-permute-start(f32[1,8,128,128]{3,2,1,0:T(8,128)S(1)} %get-tuple-element.26), channel_id=1, source_target_pairs={{0,1},{1,2},{2,3},{3,4},{4,5},{5,6},{6,7},{8,9},{9,10},{10,11},{11... | collective-permute-start | bytes 1572872 | tf_op jit(solution)/shard_map/ppermute | solution.py:16
  146.1 24.0 %copy-start.4 = (f32[2,8,128,128]{3,2,1,0:T(8,128)}, f32[2,8,128,128]{3,2,1,0:T(8,128)S(1)}, u32[]{:S(2)}) copy-start(f32[2,8,128,128]{3,2,1,0:T(8,128)S(1)} %get-tuple-element.12) | copy-start | bytes 3145732
  171.6 4.6 %copy-start.14 = (f32[2,128,127]{2,1,0:T(8,128)S(1)}, f32[2,128,127]{2,1,0:T(8,128)}, u32[]{:S(2)}) copy-start(f32[2,128,127]{2,1,0:T(8,128)} %copy-done.10) | copy-start | bytes 390148
  171.7 11.6 %collective-permute-start.12 = (f32[1,8,128,128]{3,2,1,0:T(8,128)S(1)}, f32[1,8,128,128]{3,2,1,0:T(8,128)S(1)}, u32[]{:S(2)}, u32[]{:S(2)}) collective-permute-start(f32[1,8,128,128]{3,2,1,0:T(8,128)S(1)} %get-tuple-element.25), channel_id=1, source_target_pairs={{1,0},{2,1},{3,2},{4,3},{5,4},{6,5},{7,6},{9,8},{10,9},{11,10},{12... | collective-permute-start | bytes 1572872 | tf_op jit(solution)/shard_map/ppermute | solution.py:19
  173.8 2.7 %copy-start.9 = (f32[2,127,128]{2,1,0:T(8,128)S(1)}, f32[2,127,128]{2,1,0:T(8,128)}, u32[]{:S(2)}) copy-start(f32[2,127,128]{2,1,0:T(8,128)} %copy-done.5) | copy-start | bytes 390148
  173.8 13.0 %collective-permute-start.13 = (f32[1,8,128,128]{3,2,1,0:T(8,128)S(1)}, f32[1,8,128,128]{3,2,1,0:T(8,128)S(1)}, u32[]{:S(2)}, u32[]{:S(2)}) collective-permute-start(f32[1,8,128,128]{3,2,1,0:T(8,128)S(1)} %get-tuple-element.24), channel_id=1, source_target_pairs={{0,1},{1,2},{2,3},{3,4},{4,5},{5,6},{6,7},{8,9},{9,10},{10,11},{11... | collective-permute-start | bytes 1572872 | tf_op jit(solution)/shard_map/ppermute | solution.py:16
  199.5 1.2 copy-start.2
  201.0 22.6 %collective-permute-start.14 = (f32[1,16,128,128]{3,2,1,0:T(8,128)S(1)}, f32[1,16,128,128]{3,2,1,0:T(8,128)S(1)}, u32[]{:S(2)}, u32[]{:S(2)}) collective-permute-start(f32[1,16,128,128]{3,2,1,0:T(8,128)S(1)} %get-tuple-element.22), channel_id=1, source_target_pairs={{1,0},{2,1},{3,2},{4,3},{5,4},{6,5},{7,6},{9,8},{10,9},{11,10},{12... | collective-permute-start | bytes 3145736 | tf_op jit(solution)/shard_map/ppermute | solution.py:19
  202.9 25.6 %collective-permute-start.15 = (f32[1,16,128,128]{3,2,1,0:T(8,128)S(1)}, f32[1,16,128,128]{3,2,1,0:T(8,128)S(1)}, u32[]{:S(2)}, u32[]{:S(2)}) collective-permute-start(f32[1,16,128,128]{3,2,1,0:T(8,128)S(1)} %get-tuple-element.23), channel_id=1, source_target_pairs={{0,1},{1,2},{2,3},{3,4},{4,5},{5,6},{6,7},{8,9},{9,10},{10,11},{11... | collective-permute-start | bytes 3145736 | tf_op jit(solution)/shard_map/ppermute | solution.py:16
